TPU v7x, 256 devices: a whole 4x4x8 slice. The times are simulated.
256 devices in a mesh: dp: 16 (over x, y), head: 16 (over z, core).
Axes of the slice: x: 4, y: 4, z: 8, core: 2. Of those that a mesh axis runs over, the one named last changes fastest.
Arguments:
- latents: bfloat16 [2048, 512], P('dp'), may hold values from -6 to 6
- targets: bfloat16 [2048, 32768], P('dp', 'head'), may hold values from -6 to 6
- kv_weight: bfloat16 [512, 32768], P(None, 'head'), may hold values from -0.25 to 0.25
- momentum: float32 [512, 16, 2048], P(None, 'head', 'dp'), may hold values from -120 to 120
Outputs:
- momentum_out: float32 [512, 16, 2048], P(None, 'head', 'dp')
- update: float32 [512, 16, 2048], P(None, 'head', 'dp')
All inputs are finite; a program needn't handle non-finite values.
Results may differ from a plain program's by a relative error of at most 0.0003.
The roundings to bfloat16 on the way count: a program that leaves them out, or rounds other values in their place, can miss the bound.
Values may be sent and summed in bfloat16 or wider, within the bound.
A program may use at most 64 MiB of HBM per device.

v0:
```python
import math
import jax
import jax.numpy as jnp
from jax import lax
from jax.sharding import PartitionSpec as P

C = 32768
ITERS = 2
decay_rate = 0.95
linear_coef = 3.4445
square_coef = -4.775
quint_coef = 2.0315
epsilon = 1e-07


def gram_total(iterate):
    local_gram = lax.dot_general(
        iterate, iterate, (((1,), (1,)), ((), ())), precision=lax.Precision.HIGHEST
    )
    return lax.psum(local_gram, ("dp", "head"))


def local(latents, targets, kv_weight, momentum):
    latent_width = momentum.shape[0]
    sub_width = momentum.shape[2]
    total_tokens = latents.shape[0] * lax.axis_size("dp")
    residual = (
        jnp.dot(latents, kv_weight, preferred_element_type=jnp.float32)
        - targets.astype(jnp.float32)
    ).astype(jnp.bfloat16)
    gradient = lax.psum_scatter(
        lax.dot_general(
            residual, latents, (((0,), (0,)), ((), ())), preferred_element_type=jnp.float32
        ),
        "dp",
        scatter_dimension=0,
        tiled=True,
    ).T
    gradient = gradient * (1.0 / math.sqrt(total_tokens))
    previous = momentum.reshape(latent_width, sub_width)
    momentum_new = decay_rate * previous + gradient
    nesterov = gradient + decay_rate * momentum_new
    squares = lax.psum(jnp.sum(nesterov * nesterov), ("dp", "head"))
    inverse = 1.0 / (jnp.sqrt(squares) + epsilon)
    iterate = nesterov * inverse
    gram_matrix = gram_total(iterate)
    for iteration in range(ITERS):
        if iteration > 0:
            gram_matrix = gram_total(iterate)
        polynomial = square_coef * gram_matrix + quint_coef * jnp.dot(
            gram_matrix, gram_matrix, precision=lax.Precision.HIGHEST
        )
        iterate = linear_coef * iterate + jnp.dot(
            polynomial, iterate, precision=lax.Precision.HIGHEST
        )
    update = iterate * math.sqrt(C)
    return (
        momentum_new.reshape(latent_width, 1, sub_width),
        update.reshape(latent_width, 1, sub_width),
    )


def solution(mesh):
    return jax.shard_map(
        local,
        mesh=mesh,
        in_specs=(P("dp", None), P("dp", "head"), P(None, "head"), P(None, "head", "dp")),
        out_specs=(P(None, "head", "dp"), P(None, "head", "dp")),
        check_vma=False,
    )
```

profile of v0, /device:TPU:2, one launch (start us, length us, event | category | flops | bytes accessed | tf_op | source)
XLA Modules:
  0.0 706.9 jit_solution(13692104984853528014)
XLA Ops:
  7.2 0.0 copy-start
  7.2 0.0 reduce-scatter.2.cloned.1.call-start
  7.2 1.5 copy-done
  8.8 4.0 fusion.3
  12.8 0.0 copy-start.2
  12.8 0.0 reduce-scatter.2.cloned.1.call-update
  12.8 0.0 all-reduce.3.cloned.1.call-start
  12.9 0.9 copy-done.2
  13.7 0.1 copy.6
  13.9 84.5 %reduce-scatter.2.cloned.1.call-done = f32[128,512]{1,0:T(8,128)} async-done(((f32[2048,512]{1,0:T(8,128)}), f32[128,512]{1,0:T(8,128)}) %reduce-scatter.2.cloned.1.call-update) | async-done | bytes 262160 | tf_op jit(solution)/shard_map/reduce_scatter | solution.py:31
  98.3 1.6 multiply_reduce_fusion
  99.9 73.7 %psum.21 = f32[]{:T(128)} all-reduce(f32[]{:T(128)} %get-tuple-element.4), channel_id=1, replica_groups=mesh['dp'=16,'head'=16] {'dp','head'}, use_global_device_ids=true, to_apply=%region_2.0 | all-reduce | flops 1 | bytes 8 | tf_op jit(solution)/shard_map/psum | solution.py:43
  174.3 3.1 fusion.7
  177.5 0.0 copy-start.1
  177.5 0.0 all-reduce.3.cloned.1.call-update
  177.5 0.0 all-reduce.5.cloned.1.call-start
  177.5 254.9 %all-reduce.3.cloned.1.call-done = f32[512,512]{1,0:T(8,128)} async-done(((f32[512,512]{1,0:T(8,128)}), f32[512,512]{1,0:T(8,128)}) %all-reduce.3.cloned.1.call-update) | async-done | bytes 1048592 | tf_op jit(solution)/shard_map/psum | solution.py:20
  432.5 3.9 fusion.2
  436.4 0.0 copy-done.1
  436.4 1.2 convolution_add_fusion.1
  437.6 2.1 fusion.13
  439.7 0.0 all-reduce.5.cloned.1.call-update
  439.7 0.8 copy.9
  440.6 253.9 %all-reduce.5.cloned.1.call-done = f32[512,512]{1,0:T(8,128)} async-done(((f32[512,512]{1,0:T(8,128)}), f32[512,512]{1,0:T(8,128)}) %all-reduce.5.cloned.1.call-update) | async-done | bytes 1048592 | tf_op jit(solution)/shard_map/psum | solution.py:20
  694.4 3.9 fusion.1
  698.3 1.2 fusion.5
  699.6 0.8 copy.10
Async XLA Ops:
  7.2 1.6 copy-start
  7.2 91.1 %reduce-scatter.2.cloned.1.call-start = ((), (), s32[]{:S(2)}) async-start(), calls=%async_computation.1 | async-start | bytes 4456448 | tf_op jit(solution)/shard_map/reduce_scatter | solution.py:31
  12.8 0.9 copy-start.2
  12.8 419.7 %all-reduce.3.cloned.1.call-start = ((), (), s32[]{:S(2)}) async-start(), calls=%async_computation.2 | async-start | bytes 2097152 | tf_op jit(solution)/shard_map/psum | solution.py:20
  177.5 258.9 %copy-start.1 = (f32[128,512]{1,0:T(8,128)S(1)}, f32[128,512]{1,0:T(8,128)}, u32[]{:S(2)}) copy-start(f32[128,512]{1,0:T(8,128)} %reduce-scatter.2.cloned.1.call-done) | copy-start | bytes 786436
  177.5 516.9 %all-reduce.5.cloned.1.call-start = ((), (), s32[]{:S(2)}) async-start(), calls=%async_computation.3 | async-start | bytes 2097152 | tf_op jit(solution)/shard_map/psum | solution.py:20
Sparse Core Ops, SparseCore 0:
  12.9 85.3 reduce-scatter.1
  177.6 254.8 all-reduce.2
  439.9 254.5 all-reduce.4
where the time goes:
time: 707 us
  waiting for transfers between devices  593 us (84%)
  blocking collectives  73.7 us (10%)
  matrix products  19.5 us (3%)
  between operations  14.5 us (2%)
    psum x2, waiting for transfers between devices, gram_total(): return lax.psum(local_gram, ('dp', 'head'))  509 us
    reduce_scatter x1, waiting for transfers between devices, local(): lax.psum_scatter(lax.dot_general(residual, latents, (((0,), (0,)), ((), (...  84.5 us
    psum x1, blocking collectives, local(): squares = lax.psum(jnp.sum(nesterov * nesterov), ('dp', 'head'))  73.7 us
  transfers between devices with their start and end apart: 3, of which 3 were waited for; matrix products, arithmetic and copies ran while one was open for 0% of the time, Pallas kernels for 0%

commit v1 on v0

--- a/solution.py
+++ b/solution.py
@@ -13,11 +13,17 @@
 epsilon = 1e-07
 
 
+def _return_all_floor(incoming_x, row_axis, axis_key):
+    for ii in (row_axis, axis_key):
+        incoming_x = lax.psum(incoming_x, ii)
+    return incoming_x
+
+
 def gram_total(iterate):
     local_gram = lax.dot_general(
         iterate, iterate, (((1,), (1,)), ((), ())), precision=lax.Precision.HIGHEST
     )
-    return lax.psum(local_gram, ("dp", "head"))
+    return _return_all_floor(local_gram, "head", "dp")
 
 
 def local(latents, targets, kv_weight, momentum):

time: 707 us -> 620 us (0.88)
  waiting for transfers between devices: 593 us -> 506 us
    psum x2 -> x4, waiting for transfers between devices: 509 us -> 421 us  [_return_all_floor(): incoming_x = lax.psum(incoming_x, ii)]
  transfers between devices with their start and end apart: 3 -> 5, of which waited for: 3 -> 5; matrix products, arithmetic and copies ran while one was open for 0% -> 0% of each run, Pallas kernels for 0% -> 0%
where the time goes in v1:
time: 620 us
  waiting for transfers between devices  506 us (82%)
  blocking collectives  73.7 us (12%)
  matrix products  19.9 us (3%)
  between operations  14.6 us (2%)
    psum x4, waiting for transfers between devices, _return_all_floor(): incoming_x = lax.psum(incoming_x, ii)  421 us
    reduce_scatter x1, waiting for transfers between devices, local(): lax.psum_scatter(lax.dot_general(residual, latents, (((0,), (0,)), ((), (...  84.5 us
    psum x1, blocking collectives, local(): squares = lax.psum(jnp.sum(nesterov * nesterov), ('dp', 'head'))  73.7 us
  transfers between devices with their start and end apart: 5, of which 5 were waited for; matrix products, arithmetic and copies ran while one was open for 0% of the time, Pallas kernels for 0%

profile of v1, /device:TPU:2, one launch (start us, length us, event | category | flops | bytes accessed | tf_op | source)
XLA Modules:
  0.0 619.9 jit_solution(1630520352334423915)
XLA Ops:
  7.2 0.0 copy-start
  7.2 0.0 reduce-scatter.2.cloned.1.call-start
  7.2 1.5 copy-done
  8.8 4.0 fusion.3
  12.8 0.0 copy-start.2
  12.8 0.0 reduce-scatter.2.cloned.1.call-update
  12.8 0.0 all-reduce.5.cloned.1.call-start
  12.9 0.9 copy-done.2
  13.7 0.1 copy.6
  13.9 84.5 %reduce-scatter.2.cloned.1.call-done = f32[128,512]{1,0:T(8,128)} async-done(((f32[2048,512]{1,0:T(8,128)}), f32[128,512]{1,0:T(8,128)}) %reduce-scatter.2.cloned.1.call-update) | async-done | bytes 262160 | tf_op jit(solution)/shard_map/reduce_scatter | solution.py:37
  98.3 1.6 multiply_reduce_fusion
  99.9 73.7 %psum.35 = f32[]{:T(128)} all-reduce(f32[]{:T(128)} %get-tuple-element.4), channel_id=1, replica_groups=mesh['dp'=16,'head'=16] {'dp','head'}, use_global_device_ids=true, to_apply=%region_2.0 | all-reduce | flops 1 | bytes 8 | tf_op jit(solution)/shard_map/psum | solution.py:49
  174.3 3.1 fusion.7
  177.5 0.0 all-reduce.5.cloned.1.call-update
  177.5 0.0 all-reduce.7.cloned.1.call-start
  177.5 110.3 %all-reduce.5.cloned.1.call-done = f32[512,512]{1,0:T(8,128)} async-done(((f32[512,512]{1,0:T(8,128)}), f32[512,512]{1,0:T(8,128)}) %all-reduce.5.cloned.1.call-update) | async-done | bytes 1048592 | tf_op jit(solution)/shard_map/psum | solution.py:18
  287.9 0.0 copy-start.1
  287.9 0.0 all-reduce.7.cloned.1.call-update
  287.9 0.0 all-reduce.9.cloned.1.call-start
  287.9 100.2 %all-reduce.7.cloned.1.call-done = f32[512,512]{1,0:T(8,128)} async-done(((f32[512,512]{1,0:T(8,128)}), f32[512,512]{1,0:T(8,128)}) %all-reduce.7.cloned.1.call-update) | async-done | bytes 1048592 | tf_op jit(solution)/shard_map/psum | solution.py:18
  388.1 4.1 fusion.2
  392.2 0.0 copy-done.1
  392.2 1.2 convolution_add_fusion.1
  393.5 2.1 fusion.13
  395.5 0.0 all-reduce.9.cloned.1.call-update
  395.6 0.0 all-reduce.11.cloned.1.call-start
  395.6 111.2 %all-reduce.9.cloned.1.call-done = f32[512,512]{1,0:T(8,128)} async-done(((f32[512,512]{1,0:T(8,128)}), f32[512,512]{1,0:T(8,128)}) %all-reduce.9.cloned.1.call-update) | async-done | bytes 1048592 | tf_op jit(solution)/shard_map/psum | solution.py:18
  506.8 0.0 all-reduce.11.cloned.1.call-update
  506.8 0.8 copy.9
  507.7 99.5 %all-reduce.11.cloned.1.call-done = f32[512,512]{1,0:T(8,128)} async-done(((f32[512,512]{1,0:T(8,128)}), f32[512,512]{1,0:T(8,128)}) %all-reduce.11.cloned.1.call-update) | async-done | bytes 1048592 | tf_op jit(solution)/shard_map/psum | solution.py:18
  607.2 4.1 fusion.1
  611.3 1.2 fusion.5
  612.5 0.8 copy.10
Async XLA Ops:
  7.2 1.6 copy-start
  7.2 91.1 %reduce-scatter.2.cloned.1.call-start = ((), (), s32[]{:S(2)}) async-start(), calls=%async_computation.1 | async-start | bytes 4456448 | tf_op jit(solution)/shard_map/reduce_scatter | solution.py:37
  12.8 0.9 copy-start.2
  12.8 275.1 %all-reduce.5.cloned.1.call-start = ((), (), s32[]{:S(2)}) async-start(), calls=%async_computation.2 | async-start | bytes 2097152 | tf_op jit(solution)/shard_map/psum | solution.py:18
  177.5 210.6 %all-reduce.7.cloned.1.call-start = ((), (), s32[]{:S(2)}) async-start(), calls=%async_computation.3 | async-start | bytes 2097152 | tf_op jit(solution)/shard_map/psum | solution.py:18
  287.9 104.4 %copy-start.1 = (f32[128,512]{1,0:T(8,128)S(1)}, f32[128,512]{1,0:T(8,128)}, u32[]{:S(2)}) copy-start(f32[128,512]{1,0:T(8,128)} %reduce-scatter.2.cloned.1.call-done) | copy-start | bytes 786436
  287.9 218.9 %all-reduce.9.cloned.1.call-start = ((), (), s32[]{:S(2)}) async-start(), calls=%async_computation.4 | async-start | bytes 2097152 | tf_op jit(solution)/shard_map/psum | solution.py:18
  395.6 211.6 %all-reduce.11.cloned.1.call-start = ((), (), s32[]{:S(2)}) async-start(), calls=%async_computation.5 | async-start | bytes 2097152 | tf_op jit(solution)/shard_map/psum | solution.py:18
Sparse Core Ops, SparseCore 0:
  12.9 85.3 reduce-scatter.1
  177.6 110.2 all-reduce.4
  291.1 96.9 all-reduce.6
  395.7 111.0 all-reduce.8
  510.2 96.9 all-reduce.10
